TPU v7x, 512 devices: a whole 4x4x16 slice. The times are simulated.
512 devices in a mesh: dp: 16 (over z), row: 8 (over y, core), col: 4 (over x).
Axes of the slice: x: 4, y: 4, z: 16, core: 2. Of those that a mesh axis runs over, the one named last changes fastest.
Arguments:
- grad_blocks: bfloat16 [16, 4096, 1024], P('dp', 'row', 'col'), may hold values from -300 to 300
- ln_grads: bfloat16 [16, 4, 1024], P('dp', None, 'col'), may hold values from -240 to 240, as said below
- master: float32 [4096, 1024], P(('row', 'col')), may hold values from -6 to 6
- first_moment: float32 [4096, 1024], P(('row', 'col')), may hold values from -6 to 6
- second_moment: float32 [4096, 1024], P(('row', 'col')), may hold values from 0.3 to 3
- average: float32 [4096, 1024], P('row', 'col'), may hold values from -6 to 6
- ln_master: float32 [4, 1024], P(None, 'col'), may hold values from -6 to 6
- ln_first: float32 [4, 1024], P(None, 'col'), may hold values from -6 to 6
- ln_second: float32 [4, 1024], P(None, 'col'), may hold values from 0.3 to 3
- ln_average: float32 [4, 1024], P(None, 'col'), may hold values from -6 to 6
Outputs:
- average_new: float32 [4096, 1024], P('row', 'col')
- master_new: float32 [4096, 1024], P(('row', 'col'))
- first_new: float32 [4096, 1024], P(('row', 'col'))
- second_new: float32 [4096, 1024], P(('row', 'col'))
- ln_master_new: float32 [4, 1024], P(None, 'col')
- ln_first_new: float32 [4, 1024], P(None, 'col')
- ln_second_new: float32 [4, 1024], P(None, 'col')
- ln_average_new: float32 [4, 1024], P(None, 'col')
Inputs may be any that keep to these rules, and one draw needn't show every extreme that they name: `ln_grads`: partial gradients of each data-parallel group.
All inputs are finite; a program needn't handle non-finite values.
Results may differ from a plain program's by a relative error of at most 0.0003.
Values may be sent and summed in bfloat16 or wider, within the bound.
A program may use at most 64 MiB of HBM per device.

v0:
```python
import math
import jax
import jax.numpy as jnp
from jax import lax
from jax.sharding import PartitionSpec as P

D = 1024
FF = 4096
STEP = 20
beta_one = 0.9
beta_two = 0.95
learn_rate = 0.02
decay_rate = 0.1
epsilon = 1e-08
clip_rms = 1.0
ema_keep = 0.9


def adam_step(gradient, clip_scale, first, second, master, decay_weight):
    clipped = clip_scale * gradient
    first_new = beta_one * first + (1.0 - beta_one) * clipped
    second_new = beta_two * second + (1.0 - beta_two) * clipped * clipped
    direction = (
        first_new
        / (1.0 - beta_one**STEP)
        / (jnp.sqrt(second_new / (1.0 - beta_two**STEP)) + epsilon)
    )
    master_new = master - learn_rate * (direction + decay_weight * master)
    return (master_new, first_new, second_new)


def clip_factor(norm_total):
    return jnp.minimum(1.0, clip_rms * math.sqrt(FF * D + 4 * D) / jnp.sqrt(norm_total))


def squares(gradient, ln_gradient, row_count):
    return jnp.sum(gradient * gradient) + jnp.sum(ln_gradient * ln_gradient) / row_count


def shards(
    grad_blocks,
    ln_grads,
    master,
    first_moment,
    second_moment,
    average,
    ln_master,
    ln_first,
    ln_second,
    ln_average,
):
    row_count = float(lax.axis_size("row"))
    summed, ln_gradient = lax.psum(
        (grad_blocks[0].astype(jnp.float32), ln_grads[0].astype(jnp.float32)), "dp"
    )
    gradient = lax.all_to_all(summed, "col", split_axis=0, concat_axis=1, tiled=True)
    norm_total = lax.psum(squares(gradient, ln_gradient, row_count), ("row", "col"))
    clip_scale = clip_factor(norm_total)
    master_new, first_new, second_new = adam_step(
        gradient, clip_scale, first_moment, second_moment, master, decay_rate
    )
    ln_master_new, ln_first_new, ln_second_new = adam_step(
        ln_gradient, clip_scale, ln_first, ln_second, ln_master, 0.0
    )
    ln_average_new = ema_keep * ln_average + (1.0 - ema_keep) * ln_master_new
    block_master = lax.all_to_all(master_new, "col", split_axis=1, concat_axis=0, tiled=True)
    average_new = ema_keep * average + (1.0 - ema_keep) * block_master
    return (
        average_new,
        master_new,
        first_new,
        second_new,
        ln_master_new,
        ln_first_new,
        ln_second_new,
        ln_average_new,
    )


def solution(mesh):
    placed = (
        P("dp", "row", "col"),
        P("dp", None, "col"),
        P(("row", "col"), None),
        P(("row", "col"), None),
        P(("row", "col"), None),
        P("row", "col"),
        P(None, "col"),
        P(None, "col"),
        P(None, "col"),
        P(None, "col"),
    )
    return jax.shard_map(
        shards,
        mesh=mesh,
        in_specs=placed,
        out_specs=(
            P("row", "col"),
            P(("row", "col"), None),
            P(("row", "col"), None),
            P(("row", "col"), None),
            P(None, "col"),
            P(None, "col"),
            P(None, "col"),
            P(None, "col"),
        ),
        check_vma=False,
    )
```

profile of v0, /device:TPU:2, one launch (start us, length us, event | category | flops | bytes accessed | tf_op | source)
XLA Modules:
  0.0 162.7 jit_solution(14626310819225786435)
XLA Ops:
  0.6 0.7 bitcast_convert_fusion
  1.3 69.7 %all-reduce.2 = (f32[4,128,256]{2,1,0:T(8,128)}, f32[4,256]{1,0:T(4,128)S(1)}) all-reduce(bf16[4,128,256]{2,1,0:T(8,128)(2,1)} %bitcast.20, f32[4,256]{1,0:T(4,128)S(1)} %bitcast_convert_fusion), channel_id=1, replica_groups=mesh['dp'=16,'row'=8,'col'=4] {'dp'}, use_global_device_ids=true, to_apply=%region_0.0 | all-reduce | flops 132096 | bytes 794624 | tf_op jit(solution)/shard_map/psum | solution.py:53
  71.0 0.0 copy-start.1
  71.0 5.0 %all-to-all-start = ((f32[4,128,256]{2,1,0:T(8,128)}), f32[4,128,256]{2,1,0:T(8,128)S(1)}, u32[]{:S(2)}, u32[]{:S(2)}) async-start(f32[4,128,256]{2,1,0:T(8,128)} %get-tuple-element.16), calls=%async_computation | async-start | bytes 1048576 | tf_op jit(solution)/shard_map/all_to_all | solution.py:56
  76.0 0.0 copy-done.1
  76.0 0.0 copy-start.2
  76.0 0.2 copy.24
  76.2 0.8 copy-done.2
  77.0 0.2 copy.20
  77.2 0.0 copy-start.3
  77.2 0.6 multiply_reduce_fusion.1
  78.5 4.1 %all-to-all-done = f32[4,128,256]{2,1,0:T(8,128)S(1)} async-done(((f32[4,128,256]{2,1,0:T(8,128)}), f32[4,128,256]{2,1,0:T(8,128)S(1)}, u32[]{:S(2)}, u32[]{:S(2)}) %all-to-all-start) | async-done | bytes 524320 | tf_op jit(solution)/shard_map/all_to_all | solution.py:56
  82.6 0.7 multiply_reduce_fusion
  84.0 0.0 copy-done.3
  84.0 0.2 copy.22
  84.2 64.9 %psum.23 = f32[]{:T(128)} all-reduce(f32[]{:T(128)S(6)} %add.45), channel_id=1, replica_groups=mesh['dp'=16,'row'=8,'col'=4] {'row','col'}, use_global_device_ids=true, to_apply=%region_4.0 | all-reduce | flops 1 | bytes 8 | tf_op jit(solution)/shard_map/psum | solution.py:57
  149.8 0.2 copy.21
  150.0 0.4 multiply_subtract_fusion
  150.4 1.0 copy.25
  151.4 3.7 %all-to-all-start.1 = ((f32[128,4,256]{2,0,1:T(8,128)}), f32[128,4,256]{2,0,1:T(8,128)S(1)}, u32[]{:S(2)}, u32[]{:S(2)}) async-start(f32[128,4,256]{2,0,1:T(8,128)} %copy.25), calls=%async_computation.1 | async-start | bytes 1048576 | tf_op jit(solution)/shard_map/all_to_all | solution.py:66
  155.2 1.0 copy.26
  156.2 1.0 copy.27
  157.2 0.0 copy-start.4
  157.2 1.0 copy.28
  158.2 0.0 copy-done.4
  158.2 0.0 copy-done.5
  158.2 0.0 copy-done.6
  158.2 0.0 copy-done.7
  158.2 0.6 multiply_add_fusion
  158.8 3.0 %all-to-all-done.1 = f32[128,4,256]{2,0,1:T(8,128)S(1)} async-done(((f32[128,4,256]{2,0,1:T(8,128)}), f32[128,4,256]{2,0,1:T(8,128)S(1)}, u32[]{:S(2)}, u32[]{:S(2)}) %all-to-all-start.1) | async-done | bytes 524320 | tf_op jit(solution)/shard_map/all_to_all | solution.py:66
  161.9 0.0 copy-done
  161.9 0.9 bitcast_add_fusion
  (6 shorter events, 0.1 us)
Async XLA Ops:
  71.0 5.0 %copy-start.1 = (f32[128,1024]{1,0:T(8,128)S(1)}, f32[128,1024]{1,0:T(8,128)}, u32[]{:S(2)}) copy-start(f32[128,1024]{1,0:T(8,128)} %param.12) | copy-start | bytes 1572868
  71.0 11.6 %all-to-all-start = ((f32[4,128,256]{2,1,0:T(8,128)}), f32[4,128,256]{2,1,0:T(8,128)S(1)}, u32[]{:S(2)}, u32[]{:S(2)}) async-start(f32[4,128,256]{2,1,0:T(8,128)} %get-tuple-element.16), calls=%async_computation | async-start | bytes 1048576 | tf_op jit(solution)/shard_map/all_to_all | solution.py:56
  76.0 1.0 copy-start.2
  77.2 6.8 %copy-start.3 = (f32[128,1024]{1,0:T(8,128)S(1)}, f32[128,1024]{1,0:T(8,128)}, u32[]{:S(2)}) copy-start(f32[128,1024]{1,0:T(8,128)} %param.14) | copy-start | bytes 1572868
  151.4 10.4 %all-to-all-start.1 = ((f32[128,4,256]{2,0,1:T(8,128)}), f32[128,4,256]{2,0,1:T(8,128)S(1)}, u32[]{:S(2)}, u32[]{:S(2)}) async-start(f32[128,4,256]{2,0,1:T(8,128)} %copy.25), calls=%async_computation.1 | async-start | bytes 1048576 | tf_op jit(solution)/shard_map/all_to_all | solution.py:66
  157.2 1.0 copy-start.4
  157.2 1.0 copy-start.5
  157.2 1.0 copy-start.6
  157.2 1.0 copy-start.7
  158.8 3.0 %copy-start = (f32[512,256]{1,0:T(8,128)S(1)}, f32[512,256]{1,0:T(8,128)}, u32[]{:S(2)}) copy-start(f32[512,256]{1,0:T(8,128)} %param.15) | copy-start | bytes 1572868
where the time goes:
time: 163 us
  blocking collectives  135 us (83%)
  starting transfers between devices  8.69 us (5%)
  waiting for transfers between devices  7.11 us (4%)
  local copies, waits for them, and re-layouts  5.61 us (3%)
  other arithmetic  4.02 us (2%)
  between operations  2.72 us (2%)
    psum x1, blocking collectives, shards(): lax.psum((grad_blocks[0].astype(jnp.float32), ln_grads[0].astype(jnp.floa...  69.7 us
    psum x1, blocking collectives, shards(): lax.psum(squares(gradient, ln_gradient, row_count), ('row', 'col'))  64.9 us
    all_to_all x1, starting transfers between devices, shards(): lax.all_to_all(summed, 'col', split_axis=0, concat_axis=1, tiled=True)  4.96 us
    unnamed x22, local copies, waits for them, and re-layouts  4.42 us
    all_to_all x1, waiting for transfers between devices, shards(): lax.all_to_all(summed, 'col', split_axis=0, concat_axis=1, tiled=True)  4.12 us
    all_to_all x1, starting transfers between devices, shards(): lax.all_to_all(master_new, 'col', split_axis=1, concat_axis=0, tiled=True)  3.73 us
  transfers between devices with their start and end apart: 2, of which 2 were waited for; matrix products, arithmetic and copies ran while one was open for 3% of the time, Pallas kernels for 0%

commit v1 on v0

--- a/solution.py
+++ b/solution.py
@@ -54,7 +54,9 @@
         (grad_blocks[0].astype(jnp.float32), ln_grads[0].astype(jnp.float32)), "dp"
     )
     gradient = lax.all_to_all(summed, "col", split_axis=0, concat_axis=1, tiled=True)
-    norm_total = lax.psum(squares(gradient, ln_gradient, row_count), ("row", "col"))
+    norm_total = squares(gradient, ln_gradient, row_count)
+    for name in ("row", "col"):
+        norm_total = lax.psum(norm_total, name)
     clip_scale = clip_factor(norm_total)
     master_new, first_new, second_new = adam_step(
         gradient, clip_scale, first_moment, second_moment, master, decay_rate

time: 163 us -> 122 us (0.75)
  blocking collectives: 135 us -> 92.4 us
    psum x1 -> x2, blocking collectives: 64.9 us -> 22.8 us  [shards(): norm_total = lax.psum(norm_total, name)]
  transfers between devices with their start and end apart: 2 -> 2, of which waited for: 2 -> 2; matrix products, arithmetic and copies ran while one was open for 3% -> 4% of each run, Pallas kernels for 0% -> 0%
where the time goes in v1:
time: 122 us
  blocking collectives  92.4 us (76%)
  starting transfers between devices  9.57 us (8%)
  waiting for transfers between devices  8.15 us (7%)
  local copies, waits for them, and re-layouts  4.77 us (4%)
  other arithmetic  4.02 us (3%)
  between operations  2.73 us (2%)
    psum x1, blocking collectives, shards(): lax.psum((grad_blocks[0].astype(jnp.float32), ln_grads[0].astype(jnp.floa...  69.7 us
    psum x2, blocking collectives, shards(): norm_total = lax.psum(norm_total, name)  22.8 us
    all_to_all x1, waiting for transfers between devices, shards(): lax.all_to_all(summed, 'col', split_axis=0, concat_axis=1, tiled=True)  5.16 us
    all_to_all x1, starting transfers between devices, shards(): lax.all_to_all(summed, 'col', split_axis=0, concat_axis=1, tiled=True)  4.96 us
    all_to_all x1, starting transfers between devices, shards(): lax.all_to_all(master_new, 'col', split_axis=1, concat_axis=0, tiled=True)  4.61 us
    unnamed x22, local copies, waits for them, and re-layouts  3.59 us
    all_to_all x1, waiting for transfers between devices, shards(): lax.all_to_all(master_new, 'col', split_axis=1, concat_axis=0, tiled=True)  2.99 us
  transfers between devices with their start and end apart: 2, of which 2 were waited for; matrix products, arithmetic and copies ran while one was open for 4% of the time, Pallas kernels for 0%

profile of v1, /device:TPU:2, one launch (start us, length us, event | category | flops | bytes accessed | tf_op | source)
XLA Modules:
  0.0 121.7 jit_solution(5111033221474900898)
XLA Ops:
  0.6 0.7 bitcast_convert_fusion
  1.3 69.7 %all-reduce.2 = (f32[4,128,256]{2,1,0:T(8,128)}, f32[4,256]{1,0:T(4,128)S(1)}) all-reduce(bf16[4,128,256]{2,1,0:T(8,128)(2,1)} %bitcast.20, f32[4,256]{1,0:T(4,128)S(1)} %bitcast_convert_fusion), channel_id=1, replica_groups=mesh['dp'=16,'row'=8,'col'=4] {'dp'}, use_global_device_ids=true, to_apply=%region_0.0 | all-reduce | flops 132096 | bytes 794624 | tf_op jit(solution)/shard_map/psum | solution.py:53
  71.0 0.0 copy-start.1
  71.0 5.0 %all-to-all-start = ((f32[4,128,256]{2,1,0:T(8,128)}), f32[4,128,256]{2,1,0:T(8,128)S(1)}, u32[]{:S(2)}, u32[]{:S(2)}) async-start(f32[4,128,256]{2,1,0:T(8,128)} %get-tuple-element.16), calls=%async_computation | async-start | bytes 1048576 | tf_op jit(solution)/shard_map/all_to_all | solution.py:56
  76.0 0.0 copy-done.1
  76.0 0.2 copy.24
  76.2 0.0 copy-start.2
  76.2 0.6 multiply_reduce_fusion.1
  77.4 5.2 %all-to-all-done = f32[4,128,256]{2,1,0:T(8,128)S(1)} async-done(((f32[4,128,256]{2,1,0:T(8,128)}), f32[4,128,256]{2,1,0:T(8,128)S(1)}, u32[]{:S(2)}, u32[]{:S(2)}) %all-to-all-start) | async-done | bytes 524320 | tf_op jit(solution)/shard_map/all_to_all | solution.py:56
  82.6 0.7 multiply_reduce_fusion
  84.0 0.0 copy-done.2
  84.0 0.0 copy-start.3
  84.0 0.2 copy.20
  84.2 12.9 %psum.30 = f32[]{:T(128)} all-reduce(f32[]{:T(128)S(6)} %add.47), channel_id=1, replica_groups=mesh['dp'=16,'row'=8,'col'=4] {'row'}, use_global_device_ids=true, to_apply=%region_4.0 | all-reduce | flops 1 | bytes 8 | tf_op jit(solution)/shard_map/psum | solution.py:59
  97.1 0.0 copy-done.3
  97.1 0.2 copy.22
  97.3 9.8 %psum.31 = f32[]{:T(128)} all-reduce(f32[]{:T(128)} %psum.30), channel_id=1, replica_groups=mesh['dp'=16,'row'=8,'col'=4] {'col'}, use_global_device_ids=true, to_apply=%region_5.0 | all-reduce | flops 1 | bytes 8 | tf_op jit(solution)/shard_map/psum | solution.py:59
  107.8 0.2 copy.21
  108.1 0.4 multiply_subtract_fusion
  108.5 1.0 copy.25
  109.5 4.6 %all-to-all-start.1 = ((f32[128,4,256]{2,0,1:T(8,128)}), f32[128,4,256]{2,0,1:T(8,128)S(1)}, u32[]{:S(2)}, u32[]{:S(2)}) async-start(f32[128,4,256]{2,0,1:T(8,128)} %copy.25), calls=%async_computation.1 | async-start | bytes 1048576 | tf_op jit(solution)/shard_map/all_to_all | solution.py:68
  114.1 1.0 copy.26
  115.1 1.0 copy.27
  116.1 1.0 copy.28
  117.1 0.0 copy-done.4
  117.1 0.0 copy-done.5
  117.1 0.0 copy-done.6
  117.1 0.0 copy-done.7
  117.1 0.6 multiply_add_fusion
  117.7 3.0 %all-to-all-done.1 = f32[128,4,256]{2,0,1:T(8,128)S(1)} async-done(((f32[128,4,256]{2,0,1:T(8,128)}), f32[128,4,256]{2,0,1:T(8,128)S(1)}, u32[]{:S(2)}, u32[]{:S(2)}) %all-to-all-start.1) | async-done | bytes 524320 | tf_op jit(solution)/shard_map/all_to_all | solution.py:68
  120.8 0.0 copy-done
  120.8 0.9 bitcast_add_fusion
  (7 shorter events, 0.1 us)
Async XLA Ops:
  71.0 5.0 %copy-start.1 = (f32[128,1024]{1,0:T(8,128)S(1)}, f32[128,1024]{1,0:T(8,128)}, u32[]{:S(2)}) copy-start(f32[128,1024]{1,0:T(8,128)} %param.12) | copy-start | bytes 1572868
  71.0 11.6 %all-to-all-start = ((f32[4,128,256]{2,1,0:T(8,128)}), f32[4,128,256]{2,1,0:T(8,128)S(1)}, u32[]{:S(2)}, u32[]{:S(2)}) async-start(f32[4,128,256]{2,1,0:T(8,128)} %get-tuple-element.16), calls=%async_computation | async-start | bytes 1048576 | tf_op jit(solution)/shard_map/all_to_all | solution.py:56
  76.2 7.8 %copy-start.2 = (f32[128,1024]{1,0:T(8,128)S(1)}, f32[128,1024]{1,0:T(8,128)}, u32[]{:S(2)}) copy-start(f32[128,1024]{1,0:T(8,128)} %param.13) | copy-start | bytes 1572868
  84.0 13.1 %copy-start.3 = (f32[128,1024]{1,0:T(8,128)S(1)}, f32[128,1024]{1,0:T(8,128)}, u32[]{:S(2)}) copy-start(f32[128,1024]{1,0:T(8,128)} %param.14) | copy-start | bytes 1572868
  109.5 11.2 %all-to-all-start.1 = ((f32[128,4,256]{2,0,1:T(8,128)}), f32[128,4,256]{2,0,1:T(8,128)S(1)}, u32[]{:S(2)}, u32[]{:S(2)}) async-start(f32[128,4,256]{2,0,1:T(8,128)} %copy.25), calls=%async_computation.1 | async-start | bytes 1048576 | tf_op jit(solution)/shard_map/all_to_all | solution.py:68
  116.1 1.0 copy-start.4
  116.1 1.0 copy-start.5
  116.1 1.0 copy-start.6
  116.1 1.0 copy-start.7
  117.7 3.0 %copy-start = (f32[512,256]{1,0:T(8,128)S(1)}, f32[512,256]{1,0:T(8,128)}, u32[]{:S(2)}) copy-start(f32[512,256]{1,0:T(8,128)} %param.15) | copy-start | bytes 1572868
